TPU v7x, 32 devices: a whole 2x2x4 slice. The times are simulated.
32 devices in a mesh: wide: 8 (over z, y), narrow: 4 (over x, core).
Axes of the slice: x: 2, y: 2, z: 4, core: 2. Of those that a mesh axis runs over, the one named last changes fastest.
Arguments:
- inputs: bfloat16 [32768, 768], P(('wide', 'narrow')), may hold values from -6 to 6
- w_qkv: bfloat16 [768, 2304], P(('wide', 'narrow')), may hold values from -0.21875 to 0.21875
- qv_bias: bfloat16 [1536], P(('wide', 'narrow')), may hold values from -3 to 3
- w_out: bfloat16 [768, 768], P(('wide', 'narrow')), may hold values from -0.875 to 0.875
- out_bias: bfloat16 [768], P(('wide', 'narrow')), may hold values from -3 to 3
- ln1_gain: bfloat16 [768], P(('wide', 'narrow')), may hold values from 0.5 to 1.5
- ln1_shift: bfloat16 [768], P(('wide', 'narrow')), may hold values from -3 to 3
- ln2_gain: bfloat16 [768], P(('wide', 'narrow')), may hold values from 0.5 to 1.5
- ln2_shift: bfloat16 [768], P(('wide', 'narrow')), may hold values from -3 to 3
- w_up: bfloat16 [768, 3072], P(('wide', 'narrow')), may hold values from -0.21875 to 0.21875
- up_bias: bfloat16 [3072], P(('wide', 'narrow')), may hold values from -3 to 3
- w_down: bfloat16 [3072, 768], P(('wide', 'narrow')), may hold values from -0.109375 to 0.109375
- down_bias: bfloat16 [768], P(('wide', 'narrow')), may hold values from -3 to 3
- segment_ids: int32 [64, 512], P(('wide', 'narrow')), may hold values from 0 to 10, as said below
- valid: int32 [64, 512], P(('wide', 'narrow')), may hold values from 0 to 1, as said below
- cotangent: bfloat16 [32768, 768], P(('wide', 'narrow')), may hold values from -6 to 6
Outputs:
- block_out: bfloat16 [32768, 768], P(('wide', 'narrow'))
- grad_inputs: float32 [32768, 768], P(('wide', 'narrow'))
- grad_w_qkv: float32 [768, 2304], P(('wide', 'narrow'))
- grad_qv_bias: float32 [1536], P(('wide', 'narrow'))
- grad_w_out: float32 [768, 768], P(('wide', 'narrow'))
- grad_out_bias: float32 [768], P(('wide', 'narrow'))
- grad_ln1_gain: float32 [768], P(('wide', 'narrow'))
- grad_ln1_shift: float32 [768], P(('wide', 'narrow'))
- grad_ln2_gain: float32 [768], P(('wide', 'narrow'))
- grad_ln2_shift: float32 [768], P(('wide', 'narrow'))
- grad_w_up: float32 [768, 3072], P(('wide', 'narrow'))
- grad_up_bias: float32 [3072], P(('wide', 'narrow'))
- grad_w_down: float32 [3072, 768], P(('wide', 'narrow'))
- grad_down_bias: float32 [768], P(('wide', 'narrow'))
Inputs may be any that keep to these rules, and one draw needn't show every extreme that they name: `segment_ids`: never falling along a sequence; images of exactly 49 rows numbered from 0, then the padding rows as one last segment; the first sequence holds 10 images. `valid`: 0 exactly on the padding rows at the end of each sequence.
All inputs are finite; a program needn't handle non-finite values.
Results may differ from a plain program's by a relative error of at most 0.0086.
Values may be sent and summed in bfloat16 or wider, within the bound.
A program may use at most 192 MiB of HBM per device.

v0:
```python
import functools
import jax
import jax.numpy as jnp
from jax import lax
from jax.experimental import pallas as pl
from jax.experimental.pallas import tpu as pltpu
from jax.sharding import PartitionSpec as P

HD = 64
ALL = ("wide", "narrow")

EPSILON = 1e-06


def norm_parts(rows):
    center = rows - jnp.mean(rows, axis=-1, keepdims=True)
    recip = lax.rsqrt(jnp.mean(center * center, axis=-1, keepdims=True) + EPSILON)
    return (center * recip, recip)


def norm_back(grad_h, gain, normed, recip):
    scaled = grad_h * gain
    return recip * (
        scaled
        - jnp.mean(scaled, axis=-1, keepdims=True)
        - normed * jnp.mean(scaled * normed, axis=-1, keepdims=True)
    )


def col_sum(rows):
    return jnp.sum(rows.astype(jnp.float32), axis=0)


def seg_mask(seg_col, seg_row, val_row, n):
    rows = lax.broadcasted_iota(jnp.int32, (n, n), 0)
    cols = lax.broadcasted_iota(jnp.int32, (n, n), 1)
    return (seg_col == seg_row) & ((val_row == 1) | (rows == cols))


def soft_rows(qh, kh, allowed):
    scores = lax.dot_general(qh, kh, (((1,), (1,)), ((), ())), preferred_element_type=jnp.float32)
    scores = jnp.where(allowed, scores * (1.0 / HD**0.5), -1e30)
    top = jnp.max(scores, axis=-1, keepdims=True)
    expo = jnp.exp(scores - top)
    return expo * (1.0 / jnp.sum(expo, axis=-1, keepdims=True))


def attn_fwd_kernel(q_ref, k_ref, v_ref, sc_ref, sr_ref, vr_ref, o_ref):
    n = q_ref.shape[0]
    allowed = seg_mask(sc_ref[...], sr_ref[...], vr_ref[...], n)
    outs = []
    for j in range(q_ref.shape[1] // HD):
        cols = slice(j * HD, (j + 1) * HD)
        probs = soft_rows(q_ref[:, cols], k_ref[:, cols], allowed).astype(jnp.bfloat16)
        outs.append(jnp.dot(probs, v_ref[:, cols], preferred_element_type=jnp.float32))
    o_ref[...] = jnp.concatenate(outs, axis=1).astype(o_ref.dtype)


def attn_bwd_kernel(q_ref, k_ref, v_ref, do_ref, sc_ref, sr_ref, vr_ref, dqkv_ref):
    n = q_ref.shape[0]
    width = q_ref.shape[1]
    hp = pl.program_id(1)
    model_width = dqkv_ref.shape[1] // 3
    allowed = seg_mask(sc_ref[...], sr_ref[...], vr_ref[...], n)
    dqs, dks, dvs = [], [], []
    for j in range(width // HD):
        cols = slice(j * HD, (j + 1) * HD)
        qh, kh, vh, doh = q_ref[:, cols], k_ref[:, cols], v_ref[:, cols], do_ref[:, cols]
        probs = soft_rows(qh, kh, allowed)
        dvs.append(
            lax.dot_general(probs.astype(jnp.bfloat16), doh, (((0,), (0,)), ((), ())),
                            preferred_element_type=jnp.float32)
        )
        dprobs = lax.dot_general(doh, vh, (((1,), (1,)), ((), ())), preferred_element_type=jnp.float32)
        row_term = jnp.sum(probs * dprobs, axis=-1, keepdims=True)
        dscore = jnp.where(allowed, probs * (dprobs - row_term), 0.0).astype(jnp.bfloat16)
        dqs.append(jnp.dot(dscore, kh, preferred_element_type=jnp.float32) * (1.0 / HD**0.5))
        dks.append(
            lax.dot_general(dscore, qh, (((0,), (0,)), ((), ())), preferred_element_type=jnp.float32)
            * (1.0 / HD**0.5)
        )
    at = pl.multiple_of(hp * width, width)
    dqkv_ref[:, pl.ds(at, width)] = jnp.concatenate(dqs, axis=1).astype(dqkv_ref.dtype)
    dqkv_ref[:, pl.ds(at + model_width, width)] = jnp.concatenate(dks, axis=1).astype(dqkv_ref.dtype)
    dqkv_ref[:, pl.ds(at + 2 * model_width, width)] = jnp.concatenate(dvs, axis=1).astype(dqkv_ref.dtype)


def mask_operands(segment_ids, valid):
    return (segment_ids[:, :, None], segment_ids[:, None, :], valid[:, None, :])


def attention_fwd(qkv, segment_ids, valid):
    rows, width3 = qkv.shape
    model_width = width3 // 3
    n_seq, seq_len = segment_ids.shape
    blk = 12 * HD
    n_hp = model_width // blk
    off = model_width // blk
    seg_spec = [
        pl.BlockSpec((None, seq_len, 1), lambda s, h: (s, 0, 0)),
        pl.BlockSpec((None, 1, seq_len), lambda s, h: (s, 0, 0)),
        pl.BlockSpec((None, 1, seq_len), lambda s, h: (s, 0, 0)),
    ]
    flops = 4 * n_seq * seq_len * seq_len * model_width
    return pl.pallas_call(
        attn_fwd_kernel,
        out_shape=jax.ShapeDtypeStruct((rows, model_width), jnp.bfloat16),
        grid=(n_seq, n_hp),
        in_specs=[
            pl.BlockSpec((seq_len, blk), lambda s, h: (s, h)),
            pl.BlockSpec((seq_len, blk), lambda s, h: (s, off + h)),
            pl.BlockSpec((seq_len, blk), lambda s, h: (s, 2 * off + h)),
        ]
        + seg_spec,
        out_specs=pl.BlockSpec((seq_len, blk), lambda s, h: (s, h)),
        cost_estimate=pl.CostEstimate(
            flops=flops,
            transcendentals=n_seq * seq_len * seq_len * (model_width // HD),
            bytes_accessed=qkv.size * 2 + rows * model_width * 2,
        ),
    )(qkv, qkv, qkv, *mask_operands(segment_ids, valid))


def attention_bwd(qkv, grad_o, segment_ids, valid):
    rows, width3 = qkv.shape
    model_width = width3 // 3
    n_seq, seq_len = segment_ids.shape
    blk = 6 * HD
    n_hp = model_width // blk
    off = model_width // blk
    seg_spec = [
        pl.BlockSpec((None, seq_len, 1), lambda s, h: (s, 0, 0)),
        pl.BlockSpec((None, 1, seq_len), lambda s, h: (s, 0, 0)),
        pl.BlockSpec((None, 1, seq_len), lambda s, h: (s, 0, 0)),
    ]
    flops = 10 * n_seq * seq_len * seq_len * model_width
    return pl.pallas_call(
        attn_bwd_kernel,
        out_shape=jax.ShapeDtypeStruct((rows, width3), jnp.bfloat16),
        grid=(n_seq, n_hp),
        in_specs=[
            pl.BlockSpec((seq_len, blk), lambda s, h: (s, h)),
            pl.BlockSpec((seq_len, blk), lambda s, h: (s, off + h)),
            pl.BlockSpec((seq_len, blk), lambda s, h: (s, 2 * off + h)),
            pl.BlockSpec((seq_len, blk), lambda s, h: (s, h)),
        ]
        + seg_spec,
        out_specs=pl.BlockSpec((seq_len, width3), lambda s, h: (s, 0)),
        cost_estimate=pl.CostEstimate(
            flops=flops,
            transcendentals=n_seq * seq_len * seq_len * (model_width // HD),
            bytes_accessed=qkv.size * 4 + rows * model_width * 2,
        ),
    )(qkv, qkv, qkv, grad_o, *mask_operands(segment_ids, valid))


MESH_ID = pl.DeviceIdType.MESH


def ring_maps(n_wide, n_narrow):
    n_dev = n_wide * n_narrow
    if (n_wide, n_narrow) == (8, 4):
        def pos_of(w, n):
            z, y, x, c = w // 2, w % 2, n // 2, n % 2
            q = 2 * x + (x + y) % 2
            k = 4 * q + z + (q % 2) * (3 - 2 * z)
            return 2 * k + c

        def coords_of(p):
            k, c = p // 2, p % 2
            q, r = k // 4, k % 4
            z = r + (q % 2) * (3 - 2 * r)
            x = q // 2
            y = (q % 2 + x) % 2
            return z * 2 + y, x * 2 + c

    else:
        def pos_of(w, n):
            return w * n_narrow + n

        def coords_of(p):
            return p // n_narrow, p % n_narrow

    return n_dev, pos_of, coords_of


def ring_reduce_scatter(parts, mesh_shape, after=(), collective_id=0):
    n_wide, n_narrow = mesh_shape
    n_dev, pos_of, coords_of = ring_maps(n_wide, n_narrow)
    specs = []
    for i, (a, rb, split) in enumerate(parts):
        cols = a.shape[1]
        if split:
            specs.append((i, 0, 0, cols // 2))
        else:
            specs.append((i, 0, 0, cols))
    for i, (a, rb, split) in enumerate(parts):
        if split:
            specs.append((i, 1, a.shape[1] // 2, a.shape[1] // 2))
    n_in = len(parts)
    n_after = len(after)
    n_sp = len(specs)
    last_step = n_dev - 2

    def kernel(*refs):
        ins = refs[:n_in]
        outs = refs[n_in + n_after : 2 * n_in + n_after]
        at = 2 * n_in + n_after
        bufs = refs[at : at + n_sp]
        locs = refs[at + n_sp : at + 2 * n_sp]
        send_sem, recv_sem, loc_sem, credit = refs[at + 2 * n_sp :]
        p = pos_of(lax.axis_index("wide"), lax.axis_index("narrow"))
        right = coords_of((p + 1) % n_dev)
        left = coords_of((p + n_dev - 1) % n_dev)
        nbr_send = (right, left)
        nbr_recv = (left, right)

        def rows_of(q, rb):
            cw, cn = coords_of(q % n_dev)
            start = (cw * n_narrow + cn) * rb
            if rb % 8 == 0:
                start = pl.multiple_of(start, 8)
            return pl.ds(start, rb)

        def remote(j, s):
            return pltpu.make_async_remote_copy(
                src_ref=bufs[j].at[s % 3],
                dst_ref=bufs[j].at[(s + 1) % 3],
                send_sem=send_sem.at[j, s % 3],
                recv_sem=recv_sem.at[j, (s + 1) % 3],
                device_id=nbr_send[specs[j][1]],
                device_id_type=MESH_ID,
            )

        def local(j, s):
            i, dirn, c0, cw = specs[j]
            q = (p + 2 * n_dev - s - 2) if dirn == 0 else (p + s + 2)
            return pltpu.make_async_copy(
                ins[i].at[rows_of(q, parts[i][1]), pl.ds(c0, cw)], locs[j].at[s % 2], loc_sem.at[j, s % 2]
            )

        barrier = pltpu.get_barrier_semaphore()
        for nb in (left, right):
            pl.semaphore_signal(barrier, 1, device_id=nb, device_id_type=MESH_ID)
        pl.semaphore_wait(barrier, 2)

        for j, (i, dirn, c0, cw) in enumerate(specs):
            q = p + n_dev - 1 if dirn == 0 else p + 1
            cp = pltpu.make_async_copy(
                ins[i].at[rows_of(q, parts[i][1]), pl.ds(c0, cw)], bufs[j].at[0], loc_sem.at[j, 1]
            )
            cp.start()
            cp.wait()
        for j in range(n_sp):
            remote(j, 0).start()
            local(j, 0).start()

        def step(s, carry):
            for j in range(n_sp):
                dirn = specs[j][1]
                local(j, s).wait()
                remote(j, s).wait_recv()
                nxt = (s + 1) % 3
                bufs[j][nxt] = bufs[j][nxt] + locs[j][s % 2]
                if j == 0 or specs[j - 1][1] != dirn:

                    @pl.when((s >= 1) & (s + 1 <= last_step))
                    def _():
                        pl.semaphore_wait(credit.at[dirn], 1)

                @pl.when(s + 1 <= last_step)
                def _():
                    remote(j, s + 1).start()
                    local(j, s + 1).start()

            for j in range(n_sp):
                remote(j, s).wait_send()
            for dirn in (0, 1):

                @pl.when(s <= last_step - 2)
                def _():
                    pl.semaphore_signal(
                        credit.at[dirn], 1, device_id=nbr_recv[dirn], device_id_type=MESH_ID
                    )

            return carry

        lax.fori_loop(0, last_step + 1, step, 0)
        fin = (last_step + 1) % 3
        for j, (i, dirn, c0, cw) in enumerate(specs):
            outs[i][:, pl.ds(c0, cw)] = bufs[j][fin]

    out_shape = [jax.ShapeDtypeStruct((rb, a.shape[1]), a.dtype) for (a, rb, _) in parts]
    scratch = [pltpu.VMEM((3, parts[i][1], cw), jnp.float32) for (i, _, _, cw) in specs]
    scratch += [pltpu.VMEM((2, parts[i][1], cw), jnp.float32) for (i, _, _, cw) in specs]
    scratch += [
        pltpu.SemaphoreType.DMA((n_sp, 3)),
        pltpu.SemaphoreType.DMA((n_sp, 3)),
        pltpu.SemaphoreType.DMA((n_sp, 2)),
        pltpu.SemaphoreType.REGULAR((2,)),
    ]
    total = sum(a.size * 4 for (a, _, _) in parts)
    return pl.pallas_call(
        kernel,
        out_shape=out_shape,
        in_specs=[pl.BlockSpec(memory_space=pl.ANY)] * (n_in + n_after),
        out_specs=[pl.BlockSpec(memory_space=pltpu.VMEM)] * n_in,
        scratch_shapes=scratch,
        compiler_params=pltpu.CompilerParams(
            collective_id=collective_id, has_side_effects=True, vmem_limit_bytes=48 * 1024 * 1024
        ),
        cost_estimate=pl.CostEstimate(flops=total // 4, transcendentals=0, bytes_accessed=2 * total),
    )(*[a for (a, _, _) in parts], *after)


def ring_all_gather(parts, mesh_shape, collective_id=1):
    n_wide, n_narrow = mesh_shape
    n_dev, pos_of, coords_of = ring_maps(n_wide, n_narrow)
    n_in = len(parts)
    steps = (n_dev // 2, n_dev - 1 - n_dev // 2)

    def kernel(*refs):
        ins = refs[:n_in]
        outs = refs[n_in : 2 * n_in]
        send_sem, recv_sem, loc_sem = refs[2 * n_in :]
        p = pos_of(lax.axis_index("wide"), lax.axis_index("narrow"))
        right = coords_of((p + 1) % n_dev)
        left = coords_of((p + n_dev - 1) % n_dev)
        nbr_send = (right, left)

        def rows_of(q, rb):
            cw, cn = coords_of(q % n_dev)
            return pl.ds(pl.multiple_of((cw * n_narrow + cn) * rb, rb), rb)

        def copy(i, dirn, s, q):
            view = outs[i].at[rows_of(q, parts[i].shape[0])]
            return pltpu.make_async_remote_copy(
                src_ref=view,
                dst_ref=view,
                send_sem=send_sem.at[dirn, i, s],
                recv_sem=recv_sem.at[dirn, i, s],
                device_id=nbr_send[dirn],
                device_id_type=MESH_ID,
            )

        def sent(i, dirn, s):
            return copy(i, dirn, s, (p + n_dev - s) if dirn == 0 else (p + s))

        def arriving(i, dirn, s):
            return copy(i, dirn, s, (p + n_dev - 1 - s) if dirn == 0 else (p + 1 + s))

        barrier = pltpu.get_barrier_semaphore()
        for nb in (left, right):
            pl.semaphore_signal(barrier, 1, device_id=nb, device_id_type=MESH_ID)
        pl.semaphore_wait(barrier, 2)

        for i in range(n_in):
            cp = pltpu.make_async_copy(ins[i], outs[i].at[rows_of(p, parts[i].shape[0])], loc_sem.at[i])
            cp.start()
            cp.wait()

        def step(s, carry):
            for dirn in (0, 1):

                @pl.when(s < steps[dirn])
                def _():
                    for i in range(n_in):

                        @pl.when(s >= 1)
                        def _():
                            arriving(i, dirn, s - 1).wait_recv()

                        sent(i, dirn, s).start()

            return carry

        lax.fori_loop(0, steps[0], step, 0)
        for dirn in (0, 1):
            for i in range(n_in):
                arriving(i, dirn, steps[dirn] - 1).wait_recv()

        def drain(s, carry):
            for dirn in (0, 1):

                @pl.when(s < steps[dirn])
                def _():
                    for i in range(n_in):
                        sent(i, dirn, s).wait_send()

            return carry

        lax.fori_loop(0, steps[0], drain, 0)

    out_shape = [jax.ShapeDtypeStruct((n_dev * a.shape[0], a.shape[1]), a.dtype) for a in parts]
    total = sum(n_dev * a.size * a.dtype.itemsize for a in parts)
    return pl.pallas_call(
        kernel,
        out_shape=out_shape,
        in_specs=[pl.BlockSpec(memory_space=pl.ANY)] * n_in,
        out_specs=[pl.BlockSpec(memory_space=pltpu.VMEM)] * n_in,
        scratch_shapes=[
            pltpu.SemaphoreType.DMA((2, n_in, steps[0])),
            pltpu.SemaphoreType.DMA((2, n_in, steps[0])),
            pltpu.SemaphoreType.DMA((n_in,)),
        ],
        compiler_params=pltpu.CompilerParams(collective_id=collective_id, has_side_effects=True),
        cost_estimate=pl.CostEstimate(flops=0, transcendentals=0, bytes_accessed=2 * total),
    )(*parts)


def pack_rows(pieces, width):
    flat = jnp.concatenate(pieces)
    return jnp.pad(flat, (0, width - flat.shape[0]))[None, :]


def split_owned(packed, sizes):
    out = []
    at = 0
    for size in sizes:
        out.append(packed[:, at : at + size].reshape(-1))
        at += size
    return out


def on_device(
    inputs,
    w_qkv,
    qv_bias,
    w_out,
    out_bias,
    ln1_gain,
    ln1_shift,
    ln2_gain,
    ln2_shift,
    w_up,
    up_bias,
    w_down,
    down_bias,
    segment_ids,
    valid,
    cotangent,
    mesh_shape=None,
):
    row_count = inputs.shape[0]
    model_width = inputs.shape[1]
    seq_count = segment_ids.shape[0]
    seq_len = segment_ids.shape[1]
    head_count = model_width // HD
    n_dev = mesh_shape[0] * mesh_shape[1]
    small = (qv_bias, out_bias, ln1_gain, ln1_shift, ln2_gain, ln2_shift, up_bias, down_bias)
    small_sizes = [a.shape[0] for a in small]
    n_small = sum(small_sizes)
    width_q = w_qkv.shape[1]
    rows_q = w_qkv.shape[0]
    rows_o = w_out.size // width_q
    rows_u = w_up.size // width_q
    up_view = 16
    ring_up = mesh_shape == (8, 4) and w_up.size % (2 * up_view * 128) == 0
    pieces = [w_qkv, w_out.reshape(rows_o, width_q)]
    if not ring_up:
        pieces.append(w_up.reshape(rows_u, width_q))
    attn_buf = jnp.concatenate(pieces + [pack_rows(small, width_q)], axis=0)
    attn_all = lax.all_gather(attn_buf, ALL, axis=0, tiled=False)
    qkv_full = attn_all[:, :rows_q].reshape(-1, width_q)
    out_full = attn_all[:, rows_q : rows_q + rows_o].reshape(-1, model_width)
    at = rows_q + rows_o
    if ring_up:
        up_v = w_up.reshape(up_view, -1)
        half_v = up_v.shape[1] // 2
        up_a, up_b = ring_all_gather([up_v[:, :half_v], up_v[:, half_v:]], mesh_shape)
        up_full = jnp.concatenate([up_a, up_b], axis=1).reshape(-1, w_up.shape[1])
    else:
        up_full = attn_all[:, at : at + rows_u].reshape(-1, w_up.shape[1])
        at = at + rows_u
    small_full = split_owned(attn_all[:, at, :n_small], small_sizes)
    qv_full, outb_full, gain_one, shift_one, gain_two, shift_two, upb_full, downb_full = small_full
    down_full = lax.all_gather(w_down, ALL, axis=0, tiled=True)

    gain_one = gain_one.astype(jnp.float32)
    shift_one = shift_one.astype(jnp.float32)
    qv_full = qv_full.astype(jnp.float32)
    rows = inputs.astype(jnp.float32)
    normed_one, recip_one = norm_parts(rows)
    h_one = (normed_one * gain_one + shift_one).astype(jnp.bfloat16)
    qkv_rows = jnp.dot(h_one, qkv_full, preferred_element_type=jnp.float32)
    zero_bias = jnp.zeros((model_width,), jnp.float32)
    qkv_bias = jnp.concatenate([qv_full[:model_width], zero_bias, qv_full[model_width:]])
    qkv_b = (qkv_rows + qkv_bias).astype(jnp.bfloat16)
    attended = attention_fwd(qkv_b, segment_ids, valid)
    mid_rows = (
        rows
        + jnp.dot(attended, out_full, preferred_element_type=jnp.float32)
        + outb_full.astype(jnp.float32)
    )
    gain_two = gain_two.astype(jnp.float32)
    shift_two = shift_two.astype(jnp.float32)
    normed_two, recip_two = norm_parts(mid_rows)
    h_two = (normed_two * gain_two + shift_two).astype(jnp.bfloat16)
    upper = jnp.dot(h_two, up_full, preferred_element_type=jnp.float32) + upb_full.astype(
        jnp.float32
    )
    upper = lax.optimization_barrier(upper)
    gelu_rows = jax.nn.gelu(upper, approximate=False).astype(jnp.bfloat16)
    out_rows = (
        mid_rows
        + jnp.dot(gelu_rows, down_full, preferred_element_type=jnp.float32)
        + downb_full.astype(jnp.float32)
    )
    block_out = out_rows.astype(jnp.bfloat16)
    dy_rows = cotangent.astype(jnp.float32)
    grad_wdown = jnp.einsum("tf,td->fd", gelu_rows, cotangent, preferred_element_type=jnp.float32)
    grad_bdown = col_sum(cotangent)
    grad_g = jnp.einsum("td,fd->tf", cotangent, down_full, preferred_element_type=jnp.float32)
    cdf_part = 0.5 * (1.0 + jax.scipy.special.erf(upper * 0.7071067811865476))
    pdf_part = jnp.exp(-0.5 * upper * upper) * 0.3989422804014327
    grad_u = (grad_g * (cdf_part + upper * pdf_part)).astype(jnp.bfloat16)
    grad_bup = col_sum(grad_u)
    grad_wup = jnp.einsum("td,tf->df", h_two, grad_u, preferred_element_type=jnp.float32)
    grad_h2 = jnp.einsum("tf,df->td", grad_u, up_full, preferred_element_type=jnp.float32)
    grad_g2 = jnp.sum(grad_h2 * normed_two, axis=0)
    grad_c2 = jnp.sum(grad_h2, axis=0)
    grad_mid = dy_rows + norm_back(grad_h2, gain_two, normed_two, recip_two)
    grad_a = grad_mid.astype(jnp.bfloat16)
    grad_wout = jnp.einsum("tc,td->cd", attended, grad_a, preferred_element_type=jnp.float32)
    grad_bout = col_sum(grad_a)
    grad_o = jnp.einsum("td,cd->tc", grad_a, out_full, preferred_element_type=jnp.float32).astype(
        jnp.bfloat16
    )
    grad_qkv = attention_bwd(qkv_b, grad_o, segment_ids, valid)
    grad_cols = col_sum(grad_qkv)
    grad_bqv = jnp.concatenate([grad_cols[:model_width], grad_cols[2 * model_width :]])
    grad_wqkv = jnp.einsum("td,te->de", h_one, grad_qkv, preferred_element_type=jnp.float32)
    grad_h1 = jnp.einsum("te,de->td", grad_qkv, qkv_full, preferred_element_type=jnp.float32)
    grad_g1 = jnp.sum(grad_h1 * normed_one, axis=0)
    grad_c1 = jnp.sum(grad_h1, axis=0)
    grad_inputs = grad_mid + norm_back(grad_h1, gain_one, normed_one, recip_one)

    small_grads = (grad_bqv, grad_bout, grad_g1, grad_c1, grad_g2, grad_c2, grad_bup, grad_bdown)
    owned = jnp.concatenate([g.reshape(n_dev, -1) for g in small_grads], axis=1)
    lanes = 128
    small_rows = 8 * pl.cdiv(pl.cdiv(n_small, lanes), 8)
    owned = jnp.pad(owned, ((0, 0), (0, small_rows * lanes - n_small))).reshape(-1, lanes)
    parts = [
        (grad_wqkv, w_qkv.shape[0], True),
        (grad_wout, w_out.shape[0], True),
        (grad_wup, w_up.shape[0], True),
        (owned, small_rows, False),
    ]
    down_sum = lax.psum_scatter(grad_wdown, ALL, scatter_dimension=0, tiled=True)
    if all(rb % 8 == 0 and a.shape[1] % 256 == 0 for (a, rb, _) in parts[:3]):
        sums = ring_reduce_scatter(parts, mesh_shape, after=(grad_inputs, block_out))
    else:
        sums = [lax.psum_scatter(a, ALL, scatter_dimension=0, tiled=True) for (a, _, _) in parts]
    sums = list(sums[:3]) + [down_sum] + list(sums[3:])
    small_sums = split_owned(sums[4].reshape(1, -1), small_sizes)
    bqv, bout, g1, c1, g2, c2, bup, bdown = small_sums
    return (
        block_out,
        grad_inputs,
        sums[0],
        bqv,
        sums[1],
        bout,
        g1,
        c1,
        g2,
        c2,
        sums[2],
        bup,
        sums[3],
        bdown,
    )


def solution(mesh):
    in_specs = (
        P(("wide", "narrow"), None),
        P(("wide", "narrow"), None),
        P(("wide", "narrow")),
        P(("wide", "narrow"), None),
        P(("wide", "narrow")),
        P(("wide", "narrow")),
        P(("wide", "narrow")),
        P(("wide", "narrow")),
        P(("wide", "narrow")),
        P(("wide", "narrow"), None),
        P(("wide", "narrow")),
        P(("wide", "narrow"), None),
        P(("wide", "narrow")),
        P(("wide", "narrow"), None),
        P(("wide", "narrow"), None),
        P(("wide", "narrow"), None),
    )
    out_specs = (
        P(("wide", "narrow"), None),
        P(("wide", "narrow"), None),
        P(("wide", "narrow"), None),
        P(("wide", "narrow")),
        P(("wide", "narrow"), None),
        P(("wide", "narrow")),
        P(("wide", "narrow")),
        P(("wide", "narrow")),
        P(("wide", "narrow")),
        P(("wide", "narrow")),
        P(("wide", "narrow"), None),
        P(("wide", "narrow")),
        P(("wide", "narrow"), None),
        P(("wide", "narrow")),
    )
    body = functools.partial(on_device, mesh_shape=(mesh.shape["wide"], mesh.shape["narrow"]))
    return jax.shard_map(
        body, mesh=mesh, in_specs=in_specs, out_specs=out_specs, check_vma=False
    )
```

profile of v0, /device:TPU:1, one launch (start us, length us, event | category | flops | bytes accessed | tf_op | source)
XLA Modules:
  0.0 440.2 jit_solution(14678093221507285025)
XLA Ops:
  7.3 5.5 %concatenate.23 = bf16[288]{0:T(512)(128)(2,1)S(1)} concatenate(bf16[48]{0:T(256)(128)(2,1)} %param.18, bf16[24]{0:T(256)(128)(2,1)} %param.20, bf16[24]{0:T(256)(128)(2,1)} %param.21, bf16[24]{0:T(256)(128)(2,1)} %param.22, bf16[24]{0:T(256)(128)(2,1)} %param.23, bf16[24]{0:T(256)(128)(2,1)} %param.24, bf16[96]{0:T(256)(128)(2,1)} %param.26, bf16[24]{0:T(256)(128)(2,1)} %param.28), dimensions={0} | concatenate | bytes 1152 | tf_op jit(solution)/shard_map/concatenate | solution.py:412
  12.7 0.8 reshape.212
  13.5 1.6 maximum_bitcast_fusion
  15.2 0.7 all-gather.5.cloned.1.call-update
  15.9 1.3 broadcast_in_dim.14.vr_ref
  17.2 1.3 broadcast_in_dim.13.sr_ref
  18.5 1.7 convert_reduce_fusion.2
  20.2 2.0 fusion.29
  22.2 0.1 reshape.215
  22.4 0.7 fusion.38
  23.0 1.0 copy.38.sc_ref
  24.1 68.5 %shard_map.264 = (bf16[512,2304]{1,0:T(8,128)(2,1)}, bf16[512,2304]{1,0:T(8,128)(2,1)}) custom-call(bf16[16,2304]{1,0:T(8,128)(2,1)} %get-tuple-element.38.refs_0_, bf16[16,2304]{1,0:T(8,128)(2,1)} %get-tuple-element.37.refs_1_), custom_call_target="tpu_custom_call" | custom-call | bytes 9437184 | tf_op jit(solution)/shard_map/pallas_call | solution.py:396
  92.6 4.8 %pad_maximum_fusion = bf16[512,4608]{1,0:T(8,128)(2,1)} fusion(bf16[512,2304]{1,0:T(8,128)(2,1)} %get-tuple-element.21, bf16[512,2304]{1,0:T(8,128)(2,1)} %get-tuple-element.20), kind=kLoop, calls=%fused_computation.33 | loop fusion | flops 9437184 | bytes 9437184 | tf_op jit(solution)/shard_map/concatenate | solution.py:471
  97.4 8.1 %reshape.216 = bf16[768,3072]{1,0:T(8,128)(2,1)} reshape(bf16[512,4608]{1,0:T(8,128)(2,1)} %pad_maximum_fusion) | data formatting | bytes 9437184 | tf_op jit(solution)/shard_map/reshape | solution.py:471
  105.5 1.1 slice.122
  106.6 0.1 slice_convert_fusion.1
  106.7 0.1 slice_convert_fusion
  106.8 0.1 slice.101
  106.8 0.1 slice.103
  107.0 0.1 reshape.240
  107.1 0.1 reshape.237
  107.2 0.1 reshape.234
  107.3 0.1 reshape.238
  107.3 0.1 reshape.235
  107.4 0.1 reshape.236
  107.5 1.4 reshape.214
  108.9 2.4 slice.125
  111.3 1.7 copy-done.8
  113.0 6.0 %add_convert_fusion.q_ref.k_ref.v_ref = bf16[1024,2304]{1,0:T(8,128)(2,1)} fusion(bf16[768,2304]{1,0:T(8,128)(2,1)S(1)} %bitcast.51, f32[2304]{0:T(1024)S(1)} %pad_maximum_fusion.2, bf16[1024,768]{1,0:T(8,128)(2,1)S(1)} %copy-done.3, f32[768]{0:T(1024)S(1)} %reshape.235, f32[768]{0:T(1024)S(1)} %reshape.234, f32[1024]{0:T(1024)S(1)} %add_rsqrt_fusion.1, ...), kind=kOutput, calls=%fused_computation.28 | convolution fusion | flops 3633315840 | bytes 9853952 | tf_op jit(solution)/shard_map/dot_general | solution.py:485
  119.0 21.6 %shard_map.263 = bf16[1024,768]{1,0:T(8,128)(2,1)} custom-call(bf16[1024,2304]{1,0:T(8,128)(2,1)} %add_convert_fusion.q_ref.k_ref.v_ref, bf16[1024,2304]{1,0:T(8,128)(2,1)} %add_convert_fusion.q_ref.k_ref.v_ref, bf16[1024,2304]{1,0:T(8,128)(2,1)} %add_convert_fusion.q_ref.k_ref.v_ref, s32[2,512,1]{2,1,0:T(8,128)} %copy.38.sc_ref, ...), custom_call_target="tpu_custom_call" | custom-call | flops 1610612736 | bytes 6291456 | tf_op jit(solution)/shard_map/pallas_call | solution.py:105
  140.6 3.8 fusion.41
  144.4 0.5 multiply_reduce_fusion.2
  144.9 7.9 %broadcast_add_fusion = f32[1024,3072]{1,0:T(8,128)S(1)} fusion(f32[3072]{0:T(1024)S(1)} %reshape.239, bf16[768,3072]{1,0:T(8,128)(2,1)} %reshape.216, f32[1024,768]{1,0:T(8,128)S(1)} %get-tuple-element.56, f32[768]{0:T(1024)S(1)} %reshape.238, f32[768]{0:T(1024)S(1)} %reshape.237, f32[1024]{0:T(1024)S(1)} %add_rsqrt_fusion, ...), kind=kOutput, calls=%fused_computation.29 | convolution fusion | flops 4838916096 | bytes 20473856 | tf_op jit(solution)/shard_map/dot_general | solution.py:499
  152.8 27.2 %fusion.2 = bf16[1024,3072]{1,0:T(8,128)(2,1)S(1)} fusion(f32[1024,3072]{1,0:T(8,128)S(1)} %broadcast_add_fusion), kind=kLoop, calls=%fused_computation.4 | loop fusion | flops 204472320 | bytes 18874368 | tf_op jit(solution)/shard_map/convert_element_type | solution.py:503
  180.0 2.7 copy-done.7
  182.6 7.7 %fusion.42 = f32[3072,768]{1,0:T(8,128)} fusion(bf16[1024,3072]{1,0:T(8,128)(2,1)S(1)} %fusion.2, bf16[1024,768]{1,0:T(8,128)(2,1)S(1)} %copy-done.10), kind=kOutput, calls=%fused_computation.98 | convolution fusion | flops 4831838208 | bytes 17301504 | tf_op jit(solution)/shard_map/tf,td->fd/dot_general | solution.py:511
  190.4 14.0 %convert_reduce_fusion = (f32[3072]{0:T(1024)S(1)}, bf16[1024,3072]{1,0:T(8,128)(2,1)}) fusion(f32[1024,3072]{1,0:T(8,128)} %copy-done.5, bf16[1024,768]{1,0:T(8,128)(2,1)} %param.31, bf16[3072,768]{1,0:T(8,128)(2,1)} %all-gather.5.cloned.1.call-done), kind=kOutput, calls=%fused_computation.11 | convolution fusion | flops 4869583872 | bytes 25178112 | tf_op jit(solution)/shard_map/td,fd->tf/dot_general | solution.py:513
  204.5 9.7 %multiply_reduce_fusion = (f32[768]{0:T(1024)S(1)}, f32[1024]{0:T(1024)S(1)}, f32[1024]{0:T(1024)S(1)}, f32[768]{0:T(1024)S(1)}, f32[1024,768]{1,0:T(8,128)S(1)}) fusion(f32[1024,768]{1,0:T(8,128)S(1)} %get-tuple-element.56, f32[1024]{0:T(1024)S(1)} %add_rsqrt_fusion, f32[1024]{0:T(1024)S(1)} %broadcast_multiply_fusion.4, f32[768]{0:T(1024)S(1)} %reshape.237, ...), kind=kOutput, calls=%fused_computation.51 | convolution fusion | flops 4838912000 | bytes 17327104 | tf_op jit(solution)/shard_map/tf,df->td/dot_general | solution.py:519
  214.2 2.6 convert_reduce_fusion.4
  216.9 0.1 reshape.217
  216.9 0.1 reshape.220
  217.0 0.1 reshape.223
  217.1 0.1 reshape.221
  217.2 5.0 %convolution_convert_fusion.do_ref = bf16[1024,768]{1,0:T(8,128)(2,1)} fusion(bf16[768,768]{1,0:T(8,128)(2,1)} %reshape.214, f32[1024,768]{1,0:T(8,128)} %get-tuple-element.35), kind=kOutput, calls=%fused_computation.60 | convolution fusion | flops 1209532416 | bytes 5898240 | tf_op jit(solution)/shard_map/td,cd->tc/dot_general | solution.py:526
  222.2 34.4 %shard_map.265 = bf16[1024,2304]{1,0:T(8,128)(2,1)} custom-call(bf16[1024,2304]{1,0:T(8,128)(2,1)} %add_convert_fusion.q_ref.k_ref.v_ref, bf16[1024,2304]{1,0:T(8,128)(2,1)} %add_convert_fusion.q_ref.k_ref.v_ref, bf16[1024,2304]{1,0:T(8,128)(2,1)} %add_convert_fusion.q_ref.k_ref.v_ref, bf16[1024,768]{1,0:T(8,128)(2,1)} %convolution_convert_fusion.do_ref, ...), custom_call_target="tpu_custom_call" | custom-call | flops 4026531840 | bytes 11010048 | tf_op jit(solution)/shard_map/pallas_call | solution.py:137
  256.6 9.5 %fusion.28 = (f32[768]{0:T(1024)S(1)}, f32[1024]{0:T(1024)S(1)}, f32[1024]{0:T(1024)S(1)}, f32[768]{0:T(1024)S(1)}, f32[1024,768]{1,0:T(8,128)}) fusion(bf16[1024,768]{1,0:T(8,128)(2,1)S(1)} %copy-done.4, f32[1024]{0:T(1024)S(1)} %add_rsqrt_fusion.1, f32[1024]{0:T(1024)S(1)} %broadcast_multiply_fusion.5, f32[768]{0:T(1024)S(1)} %reshape.234, ...), kind=kOutput, calls=%fused_computation.48 | convolution fusion | flops 3631739392 | bytes 13001728 | tf_op jit(solution)/shard_map/te,de->td/dot_general | solution.py:533
  266.1 0.1 reshape.218
  266.2 3.2 convert_reduce_fusion.1
  269.4 0.1 concatenate.27
  269.4 0.1 concatenate.28
  269.5 0.1 reshape.219
  269.6 0.1 concatenate.30
  269.8 3.6 fusion.31.refs_1_
  273.5 4.5 %fusion.27.refs_4_ = f32[1024,768]{1,0:T(8,128)} fusion(f32[1024,768]{1,0:T(8,128)S(1)} %copy-done.6, bf16[1024,768]{1,0:T(8,128)(2,1)S(1)} %copy-done.4, f32[1024,768]{1,0:T(8,128)} %get-tuple-element.58, f32[1024]{0:T(1024)S(1)} %broadcast_multiply_fusion, f32[1024]{0:T(1024)S(1)} %broadcast_multiply_fusion.1, f32[768]{0:T(1024)S(1)} %reshape.234, ...), kind=kLoop, calls=%fused_computation.47 | loop fusion | flops 7077888 | bytes 11029504 | tf_op jit(solution)/shard_map/add | solution.py:536
  278.0 6.2 %fusion.34.refs_0_ = f32[768,2304]{1,0:T(8,128)} fusion(bf16[1024,2304]{1,0:T(8,128)(2,1)S(1)} %bitcast.46, bf16[1024,768]{1,0:T(8,128)(2,1)S(1)} %copy-done.4, f32[768]{0:T(1024)S(1)} %reshape.235, f32[768]{0:T(1024)S(1)} %reshape.234, f32[1024]{0:T(1024)S(1)} %add_rsqrt_fusion.1, f32[1024]{0:T(1024)S(1)} %broadcast_multiply_fusion.5), kind=kOutput, calls=%fused_computation.92 | convolution fusion | flops 3628597248 | bytes 13383680 | tf_op jit(solution)/shard_map/td,te->de/dot_general | solution.py:532
  284.2 7.5 %add_convert_fusion.1.refs_5_ = bf16[1024,768]{1,0:T(8,128)(2,1)S(1)} fusion(f32[1024,768]{1,0:T(8,128)S(1)} %copy-done.2, bf16[1024,3072]{1,0:T(8,128)(2,1)S(1)} %bitcast.50, bf16[3072,768]{1,0:T(8,128)(2,1)} %all-gather.5.cloned.1.call-done, f32[768]{0:T(1024)S(1)} %reshape.240), kind=kOutput, calls=%fused_computation.54 | convolution fusion | flops 4834197504 | bytes 15731712 | tf_op jit(solution)/shard_map/dot_general | solution.py:506
  291.8 8.6 %fusion.37.refs_2_ = f32[768,3072]{1,0:T(8,128)} fusion(bf16[1024,3072]{1,0:T(8,128)(2,1)S(1)} %bitcast.48, f32[1024,768]{1,0:T(8,128)S(1)} %copy-done.2, f32[768]{0:T(1024)S(1)} %reshape.238, f32[768]{0:T(1024)S(1)} %reshape.237, f32[1024]{0:T(1024)S(1)} %add_rsqrt_fusion, f32[1024]{0:T(1024)S(1)} %broadcast_multiply_fusion.4), kind=kOutput, calls=%fused_computation.93 | convolution fusion | flops 4835770368 | bytes 18888704 | tf_op jit(solution)/shard_map/td,tf->df/dot_general | solution.py:518
  300.4 129.1 %shard_map.266 = (f32[24,2304]{1,0:T(8,128)S(1)}, f32[24,768]{1,0:T(8,128)S(1)}, f32[24,3072]{1,0:T(8,128)S(1)}, f32[8,128]{1,0:T(8,128)S(1)}) custom-call(f32[768,2304]{1,0:T(8,128)} %fusion.34.refs_0_, f32[768,768]{1,0:T(8,128)S(1)} %fusion.31.refs_1_, f32[768,3072]{1,0:T(8,128)} %fusion.37.refs_2_, f32[256,128]{1,0:T(8,128)S(1)} %reshape.224.refs_3_, ...), custom_call_target="tpu_custom_call" | custom-call | flops 4751360 | bytes 38010880 | tf_op jit(solution)/shard_map/pallas_call | solution.py:303
  429.5 0.6 slice_bitcast_fusion.1
  430.1 0.5 slice_bitcast_fusion.7
  430.6 0.6 slice_bitcast_fusion
  431.2 0.7 copy.48
  431.9 0.6 copy.49
  432.5 0.7 copy.50
  (71 shorter events, 0.5 us)
Async XLA Ops:
  7.2 15.8 %copy-start.13 = (s32[2,512]{1,0:T(2,128)S(1)}, s32[2,512]{1,0:T(2,128)}, u32[]{:S(2)}) copy-start(s32[2,512]{1,0:T(2,128)} %param.29) | copy-start | bytes 12292
  7.2 15.0 %copy-start.12 = (bf16[24,3072]{1,0:T(8,128)(2,1)S(1)}, bf16[24,3072]{1,0:T(8,128)(2,1)}, u32[]{:S(2)}) copy-start(bf16[24,3072]{1,0:T(8,128)(2,1)} %param.25) | copy-start | bytes 442372
  7.2 98.3 %all-gather.7.cloned.1.call-start = ((), (), s32[]{:S(2)}) async-start(), calls=%async_computation.3 | async-start | bytes 6082560 | tf_op jit(solution)/shard_map/all_gather | solution.py:463
  15.1 175.3 %all-gather.5.cloned.1.call-start = ((), (), s32[]{:S(2)}) async-start(), calls=%async_computation.1 | async-start | bytes 4866048 | tf_op jit(solution)/shard_map/all_gather | solution.py:477
  15.9 415.3 %reduce-scatter.2.cloned.1.call-start = ((), (), s32[]{:S(2)}) async-start(), calls=%async_computation.2 | async-start | bytes 9732096 | tf_op jit(solution)/shard_map/reduce_scatter | solution.py:549
  105.5 2.0 slice-start.6
  108.9 4.1 copy-start.3
  111.3 1.7 copy-start.8
  144.4 69.9 %copy-start.1 = (f32[1024,768]{1,0:T(8,128)}, f32[1024,768]{1,0:T(8,128)S(1)}, u32[]{:S(2)}) copy-start(f32[1024,768]{1,0:T(8,128)S(1)} %get-tuple-element.56) | copy-start | bytes 9437188
  152.7 27.2 %copy-start.5 = (f32[1024,3072]{1,0:T(8,128)}, f32[1024,3072]{1,0:T(8,128)S(1)}, u32[]{:S(2)}) copy-start(f32[1024,3072]{1,0:T(8,128)S(1)} %broadcast_add_fusion) | copy-start | bytes 37748740
  152.8 29.9 %copy-start.10 = (bf16[1024,768]{1,0:T(8,128)(2,1)S(1)}, bf16[1024,768]{1,0:T(8,128)(2,1)}, u32[]{:S(2)}) copy-start(bf16[1024,768]{1,0:T(8,128)(2,1)} %param.31) | copy-start | bytes 4718596
  179.9 2.7 copy-start.7
  204.5 9.7 %copy-start.11 = (bf16[1024,768]{1,0:T(8,128)(2,1)S(1)}, bf16[1024,768]{1,0:T(8,128)(2,1)}, u32[]{:S(2)}) copy-start(bf16[1024,768]{1,0:T(8,128)(2,1)} %param.31) | copy-start | bytes 4718596
  222.2 34.4 %copy-start.4 = (bf16[1024,768]{1,0:T(8,128)(2,1)S(1)}, bf16[1024,768]{1,0:T(8,128)(2,1)}, u32[]{:S(2)}) copy-start(bf16[1024,768]{1,0:T(8,128)(2,1)} %param.16) | copy-start | bytes 4718596
  266.1 3.7 copy-start.9
  269.8 3.6 copy-start.6
  269.8 8.1 %slice-start = ((s8[4718592]{0:T(1024)(128)(4,1)}), s8[4194304]{0:T(1024)(128)(4,1)S(1)}, s32[]{:S(2)}) async-start(s8[4718592]{0:T(1024)(128)(4,1)} %bitcast.45), calls=%async_computation.4 | async-start | bytes 8388608
  269.8 14.3 %slice-start.4 = ((s8[6291456]{0:T(1024)(128)(4,1)}), s8[4194304]{0:T(1024)(128)(4,1)S(1)}, s32[]{:S(2)}) async-start(s8[6291456]{0:T(1024)(128)(4,1)} %bitcast.49), calls=%async_computation.8 | async-start | bytes 8388608
  273.4 4.5 %slice-start.1 = ((s8[4718592]{0:T(1024)(128)(4,1)}), s8[524288]{0:T(1024)(128)(4,1)S(1)}, s32[]{:S(2)}) async-start(s8[4718592]{0:T(1024)(128)(4,1)} %bitcast.45), calls=%async_computation.5 | async-start | bytes 1048576
  273.4 10.7 %slice-start.5 = ((s8[6291456]{0:T(1024)(128)(4,1)}), s8[2097152]{0:T(1024)(128)(4,1)S(1)}, s32[]{:S(2)}) async-start(s8[6291456]{0:T(1024)(128)(4,1)} %bitcast.49), calls=%async_computation.9 | async-start | bytes 4194304
  278.0 6.2 %copy-start.2 = (f32[1024,768]{1,0:T(8,128)S(1)}, f32[1024,768]{1,0:T(8,128)}, u32[]{:S(2)}) copy-start(f32[1024,768]{1,0:T(8,128)} %copy-done.1) | copy-start | bytes 9437188
  278.0 13.8 %slice-start.2 = ((s8[6291456]{0:T(1024)(128)(4,1)}), s8[4194304]{0:T(1024)(128)(4,1)S(1)}, s32[]{:S(2)}) async-start(s8[6291456]{0:T(1024)(128)(4,1)} %bitcast.47), calls=%async_computation.6 | async-start | bytes 8388608
  284.2 7.6 %slice-start.3 = ((s8[6291456]{0:T(1024)(128)(4,1)}), s8[2097152]{0:T(1024)(128)(4,1)S(1)}, s32[]{:S(2)}) async-start(s8[6291456]{0:T(1024)(128)(4,1)} %bitcast.47), calls=%async_computation.7 | async-start | bytes 4194304
  291.8 8.6 %copy-start = (bf16[1024,768]{1,0:T(8,128)(2,1)}, bf16[1024,768]{1,0:T(8,128)(2,1)S(1)}, u32[]{:S(2)}) copy-start(bf16[1024,768]{1,0:T(8,128)(2,1)S(1)} %add_convert_fusion.1.refs_5_) | copy-start | bytes 4718596
Sparse Core Ops, SparseCore 0:
  15.3 75.2 all-gather.6
  93.4 65.2 all-gather.4
  190.5 136.9 reduce-scatter.1
where the time goes:
time: 446 us; the launch traced here: 440 us
  Pallas kernels  254 us (57%)
  matrix products  89.4 us (20%)
  other arithmetic  48.3 us (11%)
  local copies, waits for them, and re-layouts  33.3 us (7%)
  between operations  14.8 us (3%)
    pallas_call x1, Pallas kernels, ring_reduce_scatter(): pl.pallas_call(kernel, out_shape=out_shape, in_specs=[pl.BlockSpec(memory...  129 us
    pallas_call x1, Pallas kernels, ring_all_gather(): pl.pallas_call(kernel, out_shape=out_shape, in_specs=[pl.BlockSpec(memory...  68.5 us
    pallas_call x1, Pallas kernels, attention_bwd(): pl.pallas_call(attn_bwd_kernel, out_shape=jax.ShapeDtypeStruct((rows, wid...  34.4 us
    convert_element_type x1, other arithmetic, on_device(): gelu_rows = jax.nn.gelu(upper, approximate=False).astype(jnp.bfloat16)  27.2 us
    pallas_call x1, Pallas kernels, attention_fwd(): pl.pallas_call(attn_fwd_kernel, out_shape=jax.ShapeDtypeStruct((rows, mod...  21.6 us
    dot_general x1, matrix products, on_device(): jnp.einsum('td,fd->tf', cotangent, down_full, preferred_element_type=jnp....  14 us
    dot_general x1, matrix products, on_device(): jnp.einsum('tf,df->td', grad_u, up_full, preferred_element_type=jnp.float32)  9.7 us
    dot_general x1, matrix products, on_device(): jnp.einsum('te,de->td', grad_qkv, qkv_full, preferred_element_type=jnp.fl...  9.49 us
  transfers between devices with their start and end apart: 3, of which 0 were waited for; matrix products, arithmetic and copies ran while one was open for 36% of the time, Pallas kernels for 58%

commit v1 on v0

--- a/solution.py
+++ b/solution.py
@@ -125,7 +125,7 @@
     rows, width3 = qkv.shape
     model_width = width3 // 3
     n_seq, seq_len = segment_ids.shape
-    blk = 6 * HD
+    blk = 12 * HD
     n_hp = model_width // blk
     off = model_width // blk
     seg_spec = [

time: 446 us -> 445 us (level)
  transfers between devices with their start and end apart: 3 -> 3, of which waited for: 0 -> 0; matrix products, arithmetic and copies ran while one was open for 36% -> 36% of each run, Pallas kernels for 58% -> 57%
where the time goes in v1:
time: 445 us; the launch traced here: 439 us
  Pallas kernels  252 us (57%)
  matrix products  89.4 us (20%)
  other arithmetic  48.6 us (11%)
  local copies, waits for them, and re-layouts  33.3 us (7%)
  between operations  14.6 us (3%)
    pallas_call x1, Pallas kernels, ring_reduce_scatter(): pl.pallas_call(kernel, out_shape=out_shape, in_specs=[pl.BlockSpec(memory...  129 us
    pallas_call x1, Pallas kernels, ring_all_gather(): pl.pallas_call(kernel, out_shape=out_shape, in_specs=[pl.BlockSpec(memory...  68.5 us
    pallas_call x1, Pallas kernels, attention_bwd(): pl.pallas_call(attn_bwd_kernel, out_shape=jax.ShapeDtypeStruct((rows, wid...  33.5 us
    convert_element_type x1, other arithmetic, on_device(): gelu_rows = jax.nn.gelu(upper, approximate=False).astype(jnp.bfloat16)  27.4 us
    pallas_call x1, Pallas kernels, attention_fwd(): pl.pallas_call(attn_fwd_kernel, out_shape=jax.ShapeDtypeStruct((rows, mod...  21.2 us
    dot_general x1, matrix products, on_device(): jnp.einsum('td,fd->tf', cotangent, down_full, preferred_element_type=jnp....  14 us
    dot_general x1, matrix products, on_device(): jnp.einsum('tf,df->td', grad_u, up_full, preferred_element_type=jnp.float32)  9.7 us
    dot_general x1, matrix products, on_device(): jnp.einsum('te,de->td', grad_qkv, qkv_full, preferred_element_type=jnp.fl...  9.46 us
  transfers between devices with their start and end apart: 3, of which 0 were waited for; matrix products, arithmetic and copies ran while one was open for 36% of the time, Pallas kernels for 57%

profile of v1, /device:TPU:1, one launch (start us, length us, event | category | flops | bytes accessed | tf_op | source)
XLA Modules:
  0.0 439.0 jit_solution(9732022807213830384)
XLA Ops:
  7.3 5.5 %concatenate.23 = bf16[288]{0:T(512)(128)(2,1)S(1)} concatenate(bf16[48]{0:T(256)(128)(2,1)} %param.18, bf16[24]{0:T(256)(128)(2,1)} %param.20, bf16[24]{0:T(256)(128)(2,1)} %param.21, bf16[24]{0:T(256)(128)(2,1)} %param.22, bf16[24]{0:T(256)(128)(2,1)} %param.23, bf16[24]{0:T(256)(128)(2,1)} %param.24, bf16[96]{0:T(256)(128)(2,1)} %param.26, bf16[24]{0:T(256)(128)(2,1)} %param.28), dimensions={0} | concatenate | bytes 1152 | tf_op jit(solution)/shard_map/concatenate | solution.py:412
  12.7 0.8 reshape.212
  13.5 1.6 maximum_bitcast_fusion
  15.2 0.7 all-gather.5.cloned.1.call-update
  15.9 1.3 broadcast_in_dim.14.vr_ref
  17.2 1.3 broadcast_in_dim.13.sr_ref
  18.5 1.7 convert_reduce_fusion.2
  20.2 2.0 fusion.29
  22.2 0.1 reshape.215
  22.4 0.7 fusion.38
  23.0 1.0 copy.38.sc_ref
  24.1 68.5 %shard_map.264 = (bf16[512,2304]{1,0:T(8,128)(2,1)}, bf16[512,2304]{1,0:T(8,128)(2,1)}) custom-call(bf16[16,2304]{1,0:T(8,128)(2,1)} %get-tuple-element.38.refs_0_, bf16[16,2304]{1,0:T(8,128)(2,1)} %get-tuple-element.37.refs_1_), custom_call_target="tpu_custom_call" | custom-call | bytes 9437184 | tf_op jit(solution)/shard_map/pallas_call | solution.py:396
  92.6 4.8 %pad_maximum_fusion = bf16[512,4608]{1,0:T(8,128)(2,1)} fusion(bf16[512,2304]{1,0:T(8,128)(2,1)} %get-tuple-element.21, bf16[512,2304]{1,0:T(8,128)(2,1)} %get-tuple-element.20), kind=kLoop, calls=%fused_computation.33 | loop fusion | flops 9437184 | bytes 9437184 | tf_op jit(solution)/shard_map/concatenate | solution.py:471
  97.4 8.1 %reshape.216 = bf16[768,3072]{1,0:T(8,128)(2,1)} reshape(bf16[512,4608]{1,0:T(8,128)(2,1)} %pad_maximum_fusion) | data formatting | bytes 9437184 | tf_op jit(solution)/shard_map/reshape | solution.py:471
  105.5 1.1 slice.122
  106.6 0.1 slice_convert_fusion.1
  106.7 0.1 slice_convert_fusion
  106.8 0.1 slice.101
  106.8 0.1 slice.103
  107.0 0.1 reshape.240
  107.1 0.1 reshape.237
  107.2 0.1 reshape.234
  107.3 0.1 reshape.238
  107.3 0.1 reshape.235
  107.4 0.1 reshape.236
  107.5 1.4 reshape.214
  108.9 2.4 slice.125
  111.3 1.7 copy-done.8
  113.0 6.0 %add_convert_fusion.q_ref.k_ref.v_ref = bf16[1024,2304]{1,0:T(8,128)(2,1)} fusion(bf16[768,2304]{1,0:T(8,128)(2,1)S(1)} %bitcast.51, f32[2304]{0:T(1024)S(1)} %pad_maximum_fusion.2, bf16[1024,768]{1,0:T(8,128)(2,1)S(1)} %copy-done.3, f32[768]{0:T(1024)S(1)} %reshape.235, f32[768]{0:T(1024)S(1)} %reshape.234, f32[1024]{0:T(1024)S(1)} %add_rsqrt_fusion.1, ...), kind=kOutput, calls=%fused_computation.28 | convolution fusion | flops 3633315840 | bytes 9853952 | tf_op jit(solution)/shard_map/dot_general | solution.py:485
  119.0 21.2 %shard_map.263 = bf16[1024,768]{1,0:T(8,128)(2,1)} custom-call(bf16[1024,2304]{1,0:T(8,128)(2,1)} %add_convert_fusion.q_ref.k_ref.v_ref, bf16[1024,2304]{1,0:T(8,128)(2,1)} %add_convert_fusion.q_ref.k_ref.v_ref, bf16[1024,2304]{1,0:T(8,128)(2,1)} %add_convert_fusion.q_ref.k_ref.v_ref, s32[2,512,1]{2,1,0:T(8,128)} %copy.38.sc_ref, ...), custom_call_target="tpu_custom_call" | custom-call | flops 1610612736 | bytes 6291456 | tf_op jit(solution)/shard_map/pallas_call | solution.py:105
  140.2 3.8 fusion.41
  144.0 0.5 multiply_reduce_fusion.2
  144.5 7.9 %broadcast_add_fusion = f32[1024,3072]{1,0:T(8,128)S(1)} fusion(f32[3072]{0:T(1024)S(1)} %reshape.239, bf16[768,3072]{1,0:T(8,128)(2,1)} %reshape.216, f32[1024,768]{1,0:T(8,128)S(1)} %get-tuple-element.56, f32[768]{0:T(1024)S(1)} %reshape.238, f32[768]{0:T(1024)S(1)} %reshape.237, f32[1024]{0:T(1024)S(1)} %add_rsqrt_fusion, ...), kind=kOutput, calls=%fused_computation.29 | convolution fusion | flops 4838916096 | bytes 20473856 | tf_op jit(solution)/shard_map/dot_general | solution.py:499
  152.4 27.4 %fusion.2 = bf16[1024,3072]{1,0:T(8,128)(2,1)S(1)} fusion(f32[1024,3072]{1,0:T(8,128)S(1)} %broadcast_add_fusion), kind=kLoop, calls=%fused_computation.4 | loop fusion | flops 204472320 | bytes 18874368 | tf_op jit(solution)/shard_map/convert_element_type | solution.py:503
  179.8 2.7 copy-done.7
  182.5 7.7 %fusion.42 = f32[3072,768]{1,0:T(8,128)} fusion(bf16[1024,3072]{1,0:T(8,128)(2,1)S(1)} %fusion.2, bf16[1024,768]{1,0:T(8,128)(2,1)S(1)} %copy-done.10), kind=kOutput, calls=%fused_computation.98 | convolution fusion | flops 4831838208 | bytes 17301504 | tf_op jit(solution)/shard_map/tf,td->fd/dot_general | solution.py:511
  190.3 14.0 %convert_reduce_fusion = (f32[3072]{0:T(1024)S(1)}, bf16[1024,3072]{1,0:T(8,128)(2,1)}) fusion(f32[1024,3072]{1,0:T(8,128)} %copy-done.5, bf16[1024,768]{1,0:T(8,128)(2,1)} %param.31, bf16[3072,768]{1,0:T(8,128)(2,1)} %all-gather.5.cloned.1.call-done), kind=kOutput, calls=%fused_computation.11 | convolution fusion | flops 4869583872 | bytes 25178112 | tf_op jit(solution)/shard_map/td,fd->tf/dot_general | solution.py:513
  204.4 9.7 %multiply_reduce_fusion = (f32[768]{0:T(1024)S(1)}, f32[1024]{0:T(1024)S(1)}, f32[1024]{0:T(1024)S(1)}, f32[768]{0:T(1024)S(1)}, f32[1024,768]{1,0:T(8,128)S(1)}) fusion(f32[1024,768]{1,0:T(8,128)S(1)} %get-tuple-element.56, f32[1024]{0:T(1024)S(1)} %add_rsqrt_fusion, f32[1024]{0:T(1024)S(1)} %broadcast_multiply_fusion.4, f32[768]{0:T(1024)S(1)} %reshape.237, ...), kind=kOutput, calls=%fused_computation.51 | convolution fusion | flops 4838912000 | bytes 17327104 | tf_op jit(solution)/shard_map/tf,df->td/dot_general | solution.py:519
  214.1 2.6 convert_reduce_fusion.4
  216.8 0.1 reshape.217
  216.8 0.1 reshape.220
  216.9 0.1 reshape.223
  217.0 0.1 reshape.221
  217.1 5.0 %convolution_convert_fusion.do_ref = bf16[1024,768]{1,0:T(8,128)(2,1)} fusion(bf16[768,768]{1,0:T(8,128)(2,1)} %reshape.214, f32[1024,768]{1,0:T(8,128)} %get-tuple-element.35), kind=kOutput, calls=%fused_computation.60 | convolution fusion | flops 1209532416 | bytes 5898240 | tf_op jit(solution)/shard_map/td,cd->tc/dot_general | solution.py:526
  222.1 33.5 %shard_map.265 = bf16[1024,2304]{1,0:T(8,128)(2,1)} custom-call(bf16[1024,2304]{1,0:T(8,128)(2,1)} %add_convert_fusion.q_ref.k_ref.v_ref, bf16[1024,2304]{1,0:T(8,128)(2,1)} %add_convert_fusion.q_ref.k_ref.v_ref, bf16[1024,2304]{1,0:T(8,128)(2,1)} %add_convert_fusion.q_ref.k_ref.v_ref, bf16[1024,768]{1,0:T(8,128)(2,1)} %convolution_convert_fusion.do_ref, ...), custom_call_target="tpu_custom_call" | custom-call | flops 4026531840 | bytes 11010048 | tf_op jit(solution)/shard_map/pallas_call | solution.py:137
  255.6 9.5 %fusion.28 = (f32[768]{0:T(1024)S(1)}, f32[1024]{0:T(1024)S(1)}, f32[1024]{0:T(1024)S(1)}, f32[768]{0:T(1024)S(1)}, f32[1024,768]{1,0:T(8,128)}) fusion(bf16[1024,768]{1,0:T(8,128)(2,1)S(1)} %copy-done.4, f32[1024]{0:T(1024)S(1)} %add_rsqrt_fusion.1, f32[1024]{0:T(1024)S(1)} %broadcast_multiply_fusion.5, f32[768]{0:T(1024)S(1)} %reshape.234, ...), kind=kOutput, calls=%fused_computation.48 | convolution fusion | flops 3631739392 | bytes 13001728 | tf_op jit(solution)/shard_map/te,de->td/dot_general | solution.py:533
  265.1 0.1 reshape.218
  265.1 3.3 convert_reduce_fusion.1
  268.5 0.1 concatenate.27
  268.5 0.1 concatenate.28
  268.6 0.1 reshape.219
  268.7 0.1 concatenate.30
  268.9 3.6 fusion.31.refs_1_
  272.6 4.5 %fusion.27.refs_4_ = f32[1024,768]{1,0:T(8,128)} fusion(f32[1024,768]{1,0:T(8,128)S(1)} %copy-done.6, bf16[1024,768]{1,0:T(8,128)(2,1)S(1)} %copy-done.4, f32[1024,768]{1,0:T(8,128)} %get-tuple-element.58, f32[1024]{0:T(1024)S(1)} %broadcast_multiply_fusion, f32[1024]{0:T(1024)S(1)} %broadcast_multiply_fusion.1, f32[768]{0:T(1024)S(1)} %reshape.234, ...), kind=kLoop, calls=%fused_computation.47 | loop fusion | flops 7077888 | bytes 11029504 | tf_op jit(solution)/shard_map/add | solution.py:536
  277.1 6.2 %fusion.34.refs_0_ = f32[768,2304]{1,0:T(8,128)} fusion(bf16[1024,2304]{1,0:T(8,128)(2,1)S(1)} %bitcast.46, bf16[1024,768]{1,0:T(8,128)(2,1)S(1)} %copy-done.4, f32[768]{0:T(1024)S(1)} %reshape.235, f32[768]{0:T(1024)S(1)} %reshape.234, f32[1024]{0:T(1024)S(1)} %add_rsqrt_fusion.1, f32[1024]{0:T(1024)S(1)} %broadcast_multiply_fusion.5), kind=kOutput, calls=%fused_computation.92 | convolution fusion | flops 3628597248 | bytes 13383680 | tf_op jit(solution)/shard_map/td,te->de/dot_general | solution.py:532
  283.4 7.5 %add_convert_fusion.1.refs_5_ = bf16[1024,768]{1,0:T(8,128)(2,1)S(1)} fusion(f32[1024,768]{1,0:T(8,128)S(1)} %copy-done.2, bf16[1024,3072]{1,0:T(8,128)(2,1)S(1)} %bitcast.50, bf16[3072,768]{1,0:T(8,128)(2,1)} %all-gather.5.cloned.1.call-done, f32[768]{0:T(1024)S(1)} %reshape.240), kind=kOutput, calls=%fused_computation.54 | convolution fusion | flops 4834197504 | bytes 15731712 | tf_op jit(solution)/shard_map/dot_general | solution.py:506
  290.9 8.6 %fusion.37.refs_2_ = f32[768,3072]{1,0:T(8,128)} fusion(bf16[1024,3072]{1,0:T(8,128)(2,1)S(1)} %bitcast.48, f32[1024,768]{1,0:T(8,128)S(1)} %copy-done.2, f32[768]{0:T(1024)S(1)} %reshape.238, f32[768]{0:T(1024)S(1)} %reshape.237, f32[1024]{0:T(1024)S(1)} %add_rsqrt_fusion, f32[1024]{0:T(1024)S(1)} %broadcast_multiply_fusion.4), kind=kOutput, calls=%fused_computation.93 | convolution fusion | flops 4835770368 | bytes 18888704 | tf_op jit(solution)/shard_map/td,tf->df/dot_general | solution.py:518
  299.5 129.0 %shard_map.266 = (f32[24,2304]{1,0:T(8,128)S(1)}, f32[24,768]{1,0:T(8,128)S(1)}, f32[24,3072]{1,0:T(8,128)S(1)}, f32[8,128]{1,0:T(8,128)S(1)}) custom-call(f32[768,2304]{1,0:T(8,128)} %fusion.34.refs_0_, f32[768,768]{1,0:T(8,128)S(1)} %fusion.31.refs_1_, f32[768,3072]{1,0:T(8,128)} %fusion.37.refs_2_, f32[256,128]{1,0:T(8,128)S(1)} %reshape.224.refs_3_, ...), custom_call_target="tpu_custom_call" | custom-call | flops 4751360 | bytes 38010880 | tf_op jit(solution)/shard_map/pallas_call | solution.py:303
  428.5 0.6 slice_bitcast_fusion.1
  429.1 0.5 slice_bitcast_fusion.7
  429.6 0.6 slice_bitcast_fusion
  430.2 0.7 copy.48
  430.9 0.6 copy.49
  431.5 0.7 copy.50
  (71 shorter events, 0.5 us)
Async XLA Ops:
  7.2 15.8 %copy-start.13 = (s32[2,512]{1,0:T(2,128)S(1)}, s32[2,512]{1,0:T(2,128)}, u32[]{:S(2)}) copy-start(s32[2,512]{1,0:T(2,128)} %param.29) | copy-start | bytes 12292
  7.2 15.0 %copy-start.12 = (bf16[24,3072]{1,0:T(8,128)(2,1)S(1)}, bf16[24,3072]{1,0:T(8,128)(2,1)}, u32[]{:S(2)}) copy-start(bf16[24,3072]{1,0:T(8,128)(2,1)} %param.25) | copy-start | bytes 442372
  7.2 98.3 %all-gather.7.cloned.1.call-start = ((), (), s32[]{:S(2)}) async-start(), calls=%async_computation.3 | async-start | bytes 6082560 | tf_op jit(solution)/shard_map/all_gather | solution.py:463
  15.1 175.1 %all-gather.5.cloned.1.call-start = ((), (), s32[]{:S(2)}) async-start(), calls=%async_computation.1 | async-start | bytes 4866048 | tf_op jit(solution)/shard_map/all_gather | solution.py:477
  15.9 414.3 %reduce-scatter.2.cloned.1.call-start = ((), (), s32[]{:S(2)}) async-start(), calls=%async_computation.2 | async-start | bytes 9732096 | tf_op jit(solution)/shard_map/reduce_scatter | solution.py:549
  105.5 2.0 slice-start.6
  108.9 4.1 copy-start.3
  111.3 1.7 copy-start.8
  144.0 70.1 %copy-start.1 = (f32[1024,768]{1,0:T(8,128)}, f32[1024,768]{1,0:T(8,128)S(1)}, u32[]{:S(2)}) copy-start(f32[1024,768]{1,0:T(8,128)S(1)} %get-tuple-element.56) | copy-start | bytes 9437188
  152.4 27.4 %copy-start.5 = (f32[1024,3072]{1,0:T(8,128)}, f32[1024,3072]{1,0:T(8,128)S(1)}, u32[]{:S(2)}) copy-start(f32[1024,3072]{1,0:T(8,128)S(1)} %broadcast_add_fusion) | copy-start | bytes 37748740
  152.4 30.1 %copy-start.10 = (bf16[1024,768]{1,0:T(8,128)(2,1)S(1)}, bf16[1024,768]{1,0:T(8,128)(2,1)}, u32[]{:S(2)}) copy-start(bf16[1024,768]{1,0:T(8,128)(2,1)} %param.31) | copy-start | bytes 4718596
  179.8 2.7 copy-start.7
  204.4 9.7 %copy-start.11 = (bf16[1024,768]{1,0:T(8,128)(2,1)S(1)}, bf16[1024,768]{1,0:T(8,128)(2,1)}, u32[]{:S(2)}) copy-start(bf16[1024,768]{1,0:T(8,128)(2,1)} %param.31) | copy-start | bytes 4718596
  222.1 33.5 %copy-start.4 = (bf16[1024,768]{1,0:T(8,128)(2,1)S(1)}, bf16[1024,768]{1,0:T(8,128)(2,1)}, u32[]{:S(2)}) copy-start(bf16[1024,768]{1,0:T(8,128)(2,1)} %param.16) | copy-start | bytes 4718596
  265.1 3.8 copy-start.9
  268.9 3.7 copy-start.6
  268.9 8.2 %slice-start = ((s8[4718592]{0:T(1024)(128)(4,1)}), s8[4194304]{0:T(1024)(128)(4,1)S(1)}, s32[]{:S(2)}) async-start(s8[4718592]{0:T(1024)(128)(4,1)} %bitcast.45), calls=%async_computation.4 | async-start | bytes 8388608
  268.9 14.4 %slice-start.4 = ((s8[6291456]{0:T(1024)(128)(4,1)}), s8[4194304]{0:T(1024)(128)(4,1)S(1)}, s32[]{:S(2)}) async-start(s8[6291456]{0:T(1024)(128)(4,1)} %bitcast.49), calls=%async_computation.8 | async-start | bytes 8388608
  272.6 4.5 %slice-start.1 = ((s8[4718592]{0:T(1024)(128)(4,1)}), s8[524288]{0:T(1024)(128)(4,1)S(1)}, s32[]{:S(2)}) async-start(s8[4718592]{0:T(1024)(128)(4,1)} %bitcast.45), calls=%async_computation.5 | async-start | bytes 1048576
  272.6 10.7 %slice-start.5 = ((s8[6291456]{0:T(1024)(128)(4,1)}), s8[2097152]{0:T(1024)(128)(4,1)S(1)}, s32[]{:S(2)}) async-start(s8[6291456]{0:T(1024)(128)(4,1)} %bitcast.49), calls=%async_computation.9 | async-start | bytes 4194304
  277.1 6.2 %copy-start.2 = (f32[1024,768]{1,0:T(8,128)S(1)}, f32[1024,768]{1,0:T(8,128)}, u32[]{:S(2)}) copy-start(f32[1024,768]{1,0:T(8,128)} %copy-done.1) | copy-start | bytes 9437188
  277.1 13.8 %slice-start.2 = ((s8[6291456]{0:T(1024)(128)(4,1)}), s8[4194304]{0:T(1024)(128)(4,1)S(1)}, s32[]{:S(2)}) async-start(s8[6291456]{0:T(1024)(128)(4,1)} %bitcast.47), calls=%async_computation.6 | async-start | bytes 8388608
  283.3 7.6 %slice-start.3 = ((s8[6291456]{0:T(1024)(128)(4,1)}), s8[2097152]{0:T(1024)(128)(4,1)S(1)}, s32[]{:S(2)}) async-start(s8[6291456]{0:T(1024)(128)(4,1)} %bitcast.47), calls=%async_computation.7 | async-start | bytes 4194304
  290.9 8.6 %copy-start = (bf16[1024,768]{1,0:T(8,128)(2,1)}, bf16[1024,768]{1,0:T(8,128)(2,1)S(1)}, u32[]{:S(2)}) copy-start(bf16[1024,768]{1,0:T(8,128)(2,1)S(1)} %add_convert_fusion.1.refs_5_) | copy-start | bytes 4718596
Sparse Core Ops, SparseCore 0:
  15.3 75.2 all-gather.6
  93.4 65.3 all-gather.4
  190.4 137.2 reduce-scatter.1

commit v2 on v1

--- a/solution.py
+++ b/solution.py
@@ -456,20 +456,26 @@
     rows_u = w_up.size // width_q
     up_view = 16
     ring_up = mesh_shape == (8, 4) and w_up.size % (2 * up_view * 128) == 0
-    pieces = [w_qkv, w_out.reshape(rows_o, width_q)]
+    ring_up = ring_up and w_out.size % (up_view * 128) == 0 and w_up.size % (4 * up_view * 128) == 0
+    pieces = [w_qkv]
     if not ring_up:
-        pieces.append(w_up.reshape(rows_u, width_q))
+        pieces += [w_out.reshape(rows_o, width_q), w_up.reshape(rows_u, width_q)]
     attn_buf = jnp.concatenate(pieces + [pack_rows(small, width_q)], axis=0)
     attn_all = lax.all_gather(attn_buf, ALL, axis=0, tiled=False)
     qkv_full = attn_all[:, :rows_q].reshape(-1, width_q)
-    out_full = attn_all[:, rows_q : rows_q + rows_o].reshape(-1, model_width)
-    at = rows_q + rows_o
+    at = rows_q
     if ring_up:
         up_v = w_up.reshape(up_view, -1)
-        half_v = up_v.shape[1] // 2
-        up_a, up_b = ring_all_gather([up_v[:, :half_v], up_v[:, half_v:]], mesh_shape)
-        up_full = jnp.concatenate([up_a, up_b], axis=1).reshape(-1, w_up.shape[1])
+        quarter = up_v.shape[1] // 4
+        got = ring_all_gather(
+            [w_out.reshape(up_view, -1)] + [up_v[:, k * quarter : (k + 1) * quarter] for k in range(4)],
+            mesh_shape,
+        )
+        out_full = got[0].reshape(-1, model_width)
+        up_full = jnp.concatenate(got[1:], axis=1).reshape(-1, w_up.shape[1])
     else:
+        out_full = attn_all[:, at : at + rows_o].reshape(-1, model_width)
+        at = at + rows_o
         up_full = attn_all[:, at : at + rows_u].reshape(-1, w_up.shape[1])
         at = at + rows_u
     small_full = split_owned(attn_all[:, at, :n_small], small_sizes)

time: 445 us -> 451 us (1.013)
  Pallas kernels: 252 us -> 257 us
  transfers between devices with their start and end apart: 3 -> 3, of which waited for: 0 -> 0; matrix products, arithmetic and copies ran while one was open for 36% -> 36% of each run, Pallas kernels for 57% -> 58%
where the time goes in v2:
time: 451 us; the launch traced here: 445 us
  Pallas kernels  257 us (57%)
  matrix products  89.2 us (20%)
  other arithmetic  47.9 us (11%)
  local copies, waits for them, and re-layouts  34.8 us (8%)
  between operations  14.7 us (3%)
    pallas_call x1, Pallas kernels, ring_reduce_scatter(): pl.pallas_call(kernel, out_shape=out_shape, in_specs=[pl.BlockSpec(memory...  130 us
    pallas_call x1, Pallas kernels, ring_all_gather(): pl.pallas_call(kernel, out_shape=out_shape, in_specs=[pl.BlockSpec(memory...  72.6 us
    pallas_call x1, Pallas kernels, attention_bwd(): pl.pallas_call(attn_bwd_kernel, out_shape=jax.ShapeDtypeStruct((rows, wid...  33.5 us
    convert_element_type x1, other arithmetic, on_device(): gelu_rows = jax.nn.gelu(upper, approximate=False).astype(jnp.bfloat16)  27.5 us
    pallas_call x1, Pallas kernels, attention_fwd(): pl.pallas_call(attn_fwd_kernel, out_shape=jax.ShapeDtypeStruct((rows, mod...  21.1 us
    dot_general x1, matrix products, on_device(): jnp.einsum('td,fd->tf', cotangent, down_full, preferred_element_type=jnp....  14 us
    dot_general x1, matrix products, on_device(): jnp.einsum('tf,df->td', grad_u, up_full, preferred_element_type=jnp.float32)  9.71 us
    dot_general x1, matrix products, on_device(): jnp.einsum('te,de->td', grad_qkv, qkv_full, preferred_element_type=jnp.fl...  9.53 us
  transfers between devices with their start and end apart: 3, of which 0 were waited for; matrix products, arithmetic and copies ran while one was open for 36% of the time, Pallas kernels for 58%

profile of v2, /device:TPU:1, one launch (start us, length us, event | category | flops | bytes accessed | tf_op | source)
XLA Modules:
  0.0 444.7 jit_solution(551989637495758090)
XLA Ops:
  7.3 5.5 %concatenate.23 = bf16[288]{0:T(512)(128)(2,1)S(1)} concatenate(bf16[48]{0:T(256)(128)(2,1)} %param.18, bf16[24]{0:T(256)(128)(2,1)} %param.20, bf16[24]{0:T(256)(128)(2,1)} %param.21, bf16[24]{0:T(256)(128)(2,1)} %param.22, bf16[24]{0:T(256)(128)(2,1)} %param.23, bf16[24]{0:T(256)(128)(2,1)} %param.24, bf16[96]{0:T(256)(128)(2,1)} %param.26, bf16[24]{0:T(256)(128)(2,1)} %param.28), dimensions={0} | concatenate | bytes 1152 | tf_op jit(solution)/shard_map/concatenate | solution.py:412
  12.7 1.6 maximum_bitcast_fusion
  14.4 0.7 all-gather.5.cloned.1.call-update
  15.1 1.3 broadcast_in_dim.14.vr_ref
  16.4 1.3 broadcast_in_dim.13.sr_ref
  17.7 1.7 convert_reduce_fusion.2
  19.4 2.0 fusion.29
  21.4 0.7 reshape.213.refs_0_
  22.1 0.1 reshape.214
  22.2 0.7 fusion.38
  22.9 1.1 copy.38.sc_ref
  23.9 72.6 %shard_map.264 = (bf16[512,1152]{1,0:T(8,128)(2,1)}, bf16[512,1152]{1,0:T(8,128)(2,1)}, bf16[512,1152]{1,0:T(8,128)(2,1)}, bf16[512,1152]{1,0:T(8,128)(2,1)}, bf16[512,1152]{1,0:T(8,128)(2,1)}) custom-call(bf16[16,1152]{1,0:T(8,128)(2,1)} %reshape.213.refs_0_, bf16[16,1152]{1,0:T(8,128)(2,1)} %get-tuple-element.46.refs_1_, ...), custom_call_target="tpu_custom_call" | custom-call | bytes 11796480 | tf_op jit(solution)/shard_map/pallas_call | solution.py:396
  96.5 3.1 reshape.215
  99.6 4.0 pad_maximum_fusion
  103.5 8.1 %reshape.216 = bf16[768,3072]{1,0:T(8,128)(2,1)} reshape(bf16[512,4608]{1,0:T(8,128)(2,1)} %pad_maximum_fusion) | data formatting | bytes 9437184 | tf_op jit(solution)/shard_map/reshape | solution.py:475
  111.6 1.0 slice.126
  112.6 0.1 slice_convert_fusion.1
  112.7 0.1 slice_convert_fusion
  112.8 0.1 slice.104
  112.8 0.1 slice.106
  113.0 0.1 reshape.240
  113.1 0.1 reshape.237
  113.2 0.1 reshape.234
  113.2 0.1 reshape.238
  113.3 0.1 reshape.235
  113.4 0.1 reshape.236
  113.5 2.4 slice.129
  115.9 1.7 copy-done.8
  117.6 5.9 %add_convert_fusion.q_ref.k_ref.v_ref = bf16[1024,2304]{1,0:T(8,128)(2,1)} fusion(bf16[768,2304]{1,0:T(8,128)(2,1)S(1)} %bitcast.51, f32[2304]{0:T(1024)S(1)} %pad_maximum_fusion.2, bf16[1024,768]{1,0:T(8,128)(2,1)S(1)} %copy-done.3, f32[768]{0:T(1024)S(1)} %reshape.235, f32[768]{0:T(1024)S(1)} %reshape.234, f32[1024]{0:T(1024)S(1)} %add_rsqrt_fusion.1, ...), kind=kOutput, calls=%fused_computation.28 | convolution fusion | flops 3633315840 | bytes 9853952 | tf_op jit(solution)/shard_map/dot_general | solution.py:491
  123.6 21.1 %shard_map.263 = bf16[1024,768]{1,0:T(8,128)(2,1)} custom-call(bf16[1024,2304]{1,0:T(8,128)(2,1)} %add_convert_fusion.q_ref.k_ref.v_ref, bf16[1024,2304]{1,0:T(8,128)(2,1)} %add_convert_fusion.q_ref.k_ref.v_ref, bf16[1024,2304]{1,0:T(8,128)(2,1)} %add_convert_fusion.q_ref.k_ref.v_ref, s32[2,512,1]{2,1,0:T(8,128)} %copy.38.sc_ref, ...), custom_call_target="tpu_custom_call" | custom-call | flops 1610612736 | bytes 6291456 | tf_op jit(solution)/shard_map/pallas_call | solution.py:105
  144.7 3.8 fusion.41
  148.5 0.5 multiply_reduce_fusion.2
  149.0 7.9 %broadcast_add_fusion = f32[1024,3072]{1,0:T(8,128)S(1)} fusion(f32[3072]{0:T(1024)S(1)} %reshape.239, bf16[768,3072]{1,0:T(8,128)(2,1)} %reshape.216, f32[1024,768]{1,0:T(8,128)S(1)} %get-tuple-element.64, f32[768]{0:T(1024)S(1)} %reshape.238, f32[768]{0:T(1024)S(1)} %reshape.237, f32[1024]{0:T(1024)S(1)} %add_rsqrt_fusion, ...), kind=kOutput, calls=%fused_computation.29 | convolution fusion | flops 4838916096 | bytes 20473856 | tf_op jit(solution)/shard_map/dot_general | solution.py:505
  156.8 27.5 %fusion.2 = bf16[1024,3072]{1,0:T(8,128)(2,1)S(1)} fusion(f32[1024,3072]{1,0:T(8,128)S(1)} %broadcast_add_fusion), kind=kLoop, calls=%fused_computation.4 | loop fusion | flops 204472320 | bytes 18874368 | tf_op jit(solution)/shard_map/convert_element_type | solution.py:509
  184.3 2.7 copy-done.7
  187.0 7.7 %fusion.42 = f32[3072,768]{1,0:T(8,128)} fusion(bf16[1024,3072]{1,0:T(8,128)(2,1)S(1)} %fusion.2, bf16[1024,768]{1,0:T(8,128)(2,1)S(1)} %copy-done.10), kind=kOutput, calls=%fused_computation.98 | convolution fusion | flops 4831838208 | bytes 17301504 | tf_op jit(solution)/shard_map/tf,td->fd/dot_general | solution.py:517
  194.8 14.0 %convert_reduce_fusion = (f32[3072]{0:T(1024)S(1)}, bf16[1024,3072]{1,0:T(8,128)(2,1)}) fusion(f32[1024,3072]{1,0:T(8,128)} %copy-done.5, bf16[1024,768]{1,0:T(8,128)(2,1)} %param.31, bf16[3072,768]{1,0:T(8,128)(2,1)} %all-gather.5.cloned.1.call-done), kind=kOutput, calls=%fused_computation.11 | convolution fusion | flops 4869583872 | bytes 25178112 | tf_op jit(solution)/shard_map/td,fd->tf/dot_general | solution.py:519
  208.8 9.7 %multiply_reduce_fusion = (f32[768]{0:T(1024)S(1)}, f32[1024]{0:T(1024)S(1)}, f32[1024]{0:T(1024)S(1)}, f32[768]{0:T(1024)S(1)}, f32[1024,768]{1,0:T(8,128)S(1)}) fusion(f32[1024,768]{1,0:T(8,128)S(1)} %get-tuple-element.64, f32[1024]{0:T(1024)S(1)} %add_rsqrt_fusion, f32[1024]{0:T(1024)S(1)} %broadcast_multiply_fusion.4, f32[768]{0:T(1024)S(1)} %reshape.237, ...), kind=kOutput, calls=%fused_computation.51 | convolution fusion | flops 4838912000 | bytes 17327104 | tf_op jit(solution)/shard_map/tf,df->td/dot_general | solution.py:525
  218.6 2.6 convert_reduce_fusion.4
  221.2 0.1 reshape.217
  221.3 0.1 reshape.220
  221.4 0.1 reshape.223
  221.5 0.1 reshape.221
  221.6 5.0 %convolution_convert_fusion.do_ref = bf16[1024,768]{1,0:T(8,128)(2,1)} fusion(bf16[768,768]{1,0:T(8,128)(2,1)} %reshape.215, f32[1024,768]{1,0:T(8,128)} %get-tuple-element.41), kind=kOutput, calls=%fused_computation.60 | convolution fusion | flops 1209532416 | bytes 5898240 | tf_op jit(solution)/shard_map/td,cd->tc/dot_general | solution.py:532
  226.5 33.5 %shard_map.265 = bf16[1024,2304]{1,0:T(8,128)(2,1)} custom-call(bf16[1024,2304]{1,0:T(8,128)(2,1)} %add_convert_fusion.q_ref.k_ref.v_ref, bf16[1024,2304]{1,0:T(8,128)(2,1)} %add_convert_fusion.q_ref.k_ref.v_ref, bf16[1024,2304]{1,0:T(8,128)(2,1)} %add_convert_fusion.q_ref.k_ref.v_ref, bf16[1024,768]{1,0:T(8,128)(2,1)} %convolution_convert_fusion.do_ref, ...), custom_call_target="tpu_custom_call" | custom-call | flops 4026531840 | bytes 11010048 | tf_op jit(solution)/shard_map/pallas_call | solution.py:137
  260.1 9.5 %fusion.28 = (f32[768]{0:T(1024)S(1)}, f32[1024]{0:T(1024)S(1)}, f32[1024]{0:T(1024)S(1)}, f32[768]{0:T(1024)S(1)}, f32[1024,768]{1,0:T(8,128)}) fusion(bf16[1024,768]{1,0:T(8,128)(2,1)S(1)} %copy-done.4, f32[1024]{0:T(1024)S(1)} %add_rsqrt_fusion.1, f32[1024]{0:T(1024)S(1)} %broadcast_multiply_fusion.5, f32[768]{0:T(1024)S(1)} %reshape.234, ...), kind=kOutput, calls=%fused_computation.48 | convolution fusion | flops 3631739392 | bytes 13001728 | tf_op jit(solution)/shard_map/te,de->td/dot_general | solution.py:539
  269.6 0.1 reshape.218
  269.7 3.3 convert_reduce_fusion.1
  273.0 0.1 concatenate.27
  273.1 0.1 concatenate.28
  273.2 0.1 reshape.219
  273.3 0.1 concatenate.30
  273.5 3.5 fusion.31.refs_1_
  277.0 4.6 %fusion.27.refs_4_ = f32[1024,768]{1,0:T(8,128)} fusion(f32[1024,768]{1,0:T(8,128)S(1)} %copy-done.6, bf16[1024,768]{1,0:T(8,128)(2,1)S(1)} %copy-done.4, f32[1024,768]{1,0:T(8,128)} %get-tuple-element.66, f32[1024]{0:T(1024)S(1)} %broadcast_multiply_fusion, f32[1024]{0:T(1024)S(1)} %broadcast_multiply_fusion.1, f32[768]{0:T(1024)S(1)} %reshape.234, ...), kind=kLoop, calls=%fused_computation.47 | loop fusion | flops 7077888 | bytes 11029504 | tf_op jit(solution)/shard_map/add | solution.py:542
  281.7 6.2 %fusion.34.refs_0_ = f32[768,2304]{1,0:T(8,128)} fusion(bf16[1024,2304]{1,0:T(8,128)(2,1)S(1)} %bitcast.46, bf16[1024,768]{1,0:T(8,128)(2,1)S(1)} %copy-done.4, f32[768]{0:T(1024)S(1)} %reshape.235, f32[768]{0:T(1024)S(1)} %reshape.234, f32[1024]{0:T(1024)S(1)} %add_rsqrt_fusion.1, f32[1024]{0:T(1024)S(1)} %broadcast_multiply_fusion.5), kind=kOutput, calls=%fused_computation.92 | convolution fusion | flops 3628597248 | bytes 13383680 | tf_op jit(solution)/shard_map/td,te->de/dot_general | solution.py:538
  287.9 7.5 %add_convert_fusion.1.refs_5_ = bf16[1024,768]{1,0:T(8,128)(2,1)S(1)} fusion(f32[1024,768]{1,0:T(8,128)S(1)} %copy-done.2, bf16[1024,3072]{1,0:T(8,128)(2,1)S(1)} %bitcast.50, bf16[3072,768]{1,0:T(8,128)(2,1)} %all-gather.5.cloned.1.call-done, f32[768]{0:T(1024)S(1)} %reshape.240), kind=kOutput, calls=%fused_computation.54 | convolution fusion | flops 4834197504 | bytes 15731712 | tf_op jit(solution)/shard_map/dot_general | solution.py:512
  295.5 8.6 %fusion.37.refs_2_ = f32[768,3072]{1,0:T(8,128)} fusion(bf16[1024,3072]{1,0:T(8,128)(2,1)S(1)} %bitcast.48, f32[1024,768]{1,0:T(8,128)S(1)} %copy-done.2, f32[768]{0:T(1024)S(1)} %reshape.238, f32[768]{0:T(1024)S(1)} %reshape.237, f32[1024]{0:T(1024)S(1)} %add_rsqrt_fusion, f32[1024]{0:T(1024)S(1)} %broadcast_multiply_fusion.4), kind=kOutput, calls=%fused_computation.93 | convolution fusion | flops 4835770368 | bytes 18888704 | tf_op jit(solution)/shard_map/td,tf->df/dot_general | solution.py:524
  304.1 129.9 %shard_map.266 = (f32[24,2304]{1,0:T(8,128)S(1)}, f32[24,768]{1,0:T(8,128)S(1)}, f32[24,3072]{1,0:T(8,128)S(1)}, f32[8,128]{1,0:T(8,128)S(1)}) custom-call(f32[768,2304]{1,0:T(8,128)} %fusion.34.refs_0_, f32[768,768]{1,0:T(8,128)S(1)} %fusion.31.refs_1_, f32[768,3072]{1,0:T(8,128)} %fusion.37.refs_2_, f32[256,128]{1,0:T(8,128)S(1)} %reshape.224.refs_3_, ...), custom_call_target="tpu_custom_call" | custom-call | flops 4751360 | bytes 38010880 | tf_op jit(solution)/shard_map/pallas_call | solution.py:303
  434.0 0.6 slice_bitcast_fusion.1
  434.6 0.5 slice_bitcast_fusion.7
  435.1 0.6 slice_bitcast_fusion
  435.7 0.7 copy.48
  436.4 0.6 copy.49
  437.0 0.7 copy.50
  (71 shorter events, 0.5 us)
Async XLA Ops:
  7.2 15.7 %copy-start.14 = (s32[2,512]{1,0:T(2,128)S(1)}, s32[2,512]{1,0:T(2,128)}, u32[]{:S(2)}) copy-start(s32[2,512]{1,0:T(2,128)} %param.29) | copy-start | bytes 12292
  7.2 14.2 %copy-start.13 = (bf16[24,768]{1,0:T(8,128)(2,1)S(1)}, bf16[24,768]{1,0:T(8,128)(2,1)}, u32[]{:S(2)}) copy-start(bf16[24,768]{1,0:T(8,128)(2,1)} %param.19) | copy-start | bytes 110596
  7.2 14.9 %copy-start.12 = (bf16[24,3072]{1,0:T(8,128)(2,1)S(1)}, bf16[24,3072]{1,0:T(8,128)(2,1)}, u32[]{:S(2)}) copy-start(bf16[24,3072]{1,0:T(8,128)(2,1)} %param.25) | copy-start | bytes 442372
  7.2 104.4 %all-gather.7.cloned.1.call-start = ((), (), s32[]{:S(2)}) async-start(), calls=%async_computation.3 | async-start | bytes 4866048 | tf_op jit(solution)/shard_map/all_gather | solution.py:464
  14.3 180.4 %all-gather.5.cloned.1.call-start = ((), (), s32[]{:S(2)}) async-start(), calls=%async_computation.1 | async-start | bytes 4866048 | tf_op jit(solution)/shard_map/all_gather | solution.py:483
  15.1 420.6 %reduce-scatter.2.cloned.1.call-start = ((), (), s32[]{:S(2)}) async-start(), calls=%async_computation.2 | async-start | bytes 9732096 | tf_op jit(solution)/shard_map/reduce_scatter | solution.py:555
  113.5 4.1 copy-start.3
  115.9 1.7 copy-start.8
  148.4 70.1 %copy-start.1 = (f32[1024,768]{1,0:T(8,128)}, f32[1024,768]{1,0:T(8,128)S(1)}, u32[]{:S(2)}) copy-start(f32[1024,768]{1,0:T(8,128)S(1)} %get-tuple-element.64) | copy-start | bytes 9437188
  156.8 27.5 %copy-start.5 = (f32[1024,3072]{1,0:T(8,128)}, f32[1024,3072]{1,0:T(8,128)S(1)}, u32[]{:S(2)}) copy-start(f32[1024,3072]{1,0:T(8,128)S(1)} %broadcast_add_fusion) | copy-start | bytes 37748740
  156.8 30.2 %copy-start.10 = (bf16[1024,768]{1,0:T(8,128)(2,1)S(1)}, bf16[1024,768]{1,0:T(8,128)(2,1)}, u32[]{:S(2)}) copy-start(bf16[1024,768]{1,0:T(8,128)(2,1)} %param.31) | copy-start | bytes 4718596
  184.3 2.7 copy-start.7
  208.8 9.7 %copy-start.11 = (bf16[1024,768]{1,0:T(8,128)(2,1)S(1)}, bf16[1024,768]{1,0:T(8,128)(2,1)}, u32[]{:S(2)}) copy-start(bf16[1024,768]{1,0:T(8,128)(2,1)} %param.31) | copy-start | bytes 4718596
  226.5 33.6 %copy-start.4 = (bf16[1024,768]{1,0:T(8,128)(2,1)S(1)}, bf16[1024,768]{1,0:T(8,128)(2,1)}, u32[]{:S(2)}) copy-start(bf16[1024,768]{1,0:T(8,128)(2,1)} %param.16) | copy-start | bytes 4718596
  269.6 3.8 copy-start.9
  273.5 3.5 copy-start.6
  273.5 8.2 %slice-start = ((s8[4718592]{0:T(1024)(128)(4,1)}), s8[4194304]{0:T(1024)(128)(4,1)S(1)}, s32[]{:S(2)}) async-start(s8[4718592]{0:T(1024)(128)(4,1)} %bitcast.45), calls=%async_computation.4 | async-start | bytes 8388608
  273.5 14.4 %slice-start.4 = ((s8[6291456]{0:T(1024)(128)(4,1)}), s8[4194304]{0:T(1024)(128)(4,1)S(1)}, s32[]{:S(2)}) async-start(s8[6291456]{0:T(1024)(128)(4,1)} %bitcast.49), calls=%async_computation.8 | async-start | bytes 8388608
  277.0 4.6 %slice-start.1 = ((s8[4718592]{0:T(1024)(128)(4,1)}), s8[524288]{0:T(1024)(128)(4,1)S(1)}, s32[]{:S(2)}) async-start(s8[4718592]{0:T(1024)(128)(4,1)} %bitcast.45), calls=%async_computation.5 | async-start | bytes 1048576
  277.0 10.9 %slice-start.5 = ((s8[6291456]{0:T(1024)(128)(4,1)}), s8[2097152]{0:T(1024)(128)(4,1)S(1)}, s32[]{:S(2)}) async-start(s8[6291456]{0:T(1024)(128)(4,1)} %bitcast.49), calls=%async_computation.9 | async-start | bytes 4194304
  281.6 6.2 %copy-start.2 = (f32[1024,768]{1,0:T(8,128)S(1)}, f32[1024,768]{1,0:T(8,128)}, u32[]{:S(2)}) copy-start(f32[1024,768]{1,0:T(8,128)} %copy-done.1) | copy-start | bytes 9437188
  281.6 13.8 %slice-start.2 = ((s8[6291456]{0:T(1024)(128)(4,1)}), s8[4194304]{0:T(1024)(128)(4,1)S(1)}, s32[]{:S(2)}) async-start(s8[6291456]{0:T(1024)(128)(4,1)} %bitcast.47), calls=%async_computation.6 | async-start | bytes 8388608
  287.9 7.6 %slice-start.3 = ((s8[6291456]{0:T(1024)(128)(4,1)}), s8[2097152]{0:T(1024)(128)(4,1)S(1)}, s32[]{:S(2)}) async-start(s8[6291456]{0:T(1024)(128)(4,1)} %bitcast.47), calls=%async_computation.7 | async-start | bytes 4194304
  295.5 8.6 %copy-start = (bf16[1024,768]{1,0:T(8,128)(2,1)}, bf16[1024,768]{1,0:T(8,128)(2,1)S(1)}, u32[]{:S(2)}) copy-start(bf16[1024,768]{1,0:T(8,128)(2,1)S(1)} %add_convert_fusion.1.refs_5_) | copy-start | bytes 4718596
Sparse Core Ops, SparseCore 0:
  14.5 70.1 all-gather.6
  87.5 64.1 all-gather.4
  194.9 137.5 reduce-scatter.1
